TPU v7x, 32 devices: a whole 2x2x4 slice. The times are simulated.
32 devices in a mesh: row: 8 (over z, y), col: 4 (over x, core).
Axes of the slice: x: 2, y: 2, z: 4, core: 2. Of those that a mesh axis runs over, the one named last changes fastest.
Arguments:
- examples: bfloat16 [8192, 1024], P('row'), may hold values from -40 to 40
- targets: float32 [8192, 64], P('row'), may hold values from -6 to 6
- landmark_rows: int32 [8192], P('col'), may hold values from 0 to 1023
- ainv: float32 [4, 8, 256, 8192], P(None, 'row', None, 'col'), as said below
- tinv_t: float32 [4, 8, 256, 8192], P(None, 'row', None, 'col'), as said below
Outputs:
- solution: float32 [8192, 64], P('col')
- weights: float32 [8192, 64], P('col')
Inputs may be any that keep to these rules, and one draw needn't show every extreme that they name: `landmark_rows`: landmark m is a row of example block ((m mod 2048) // 256); the value is its place within that block. `ainv`: the preconditioner's factor A inverse, in landmark order. `tinv_t`: the preconditioner's factor T inverse, transposed, in landmark order.
All inputs are finite; a program needn't handle non-finite values.
Results may differ from a plain program's by a relative error of at most 0.0003.
Values may be sent and summed in bfloat16 or wider, within the bound.
A program may use at most 128 MiB of HBM per device.

v0:
```python
import math

import jax
import jax.numpy as jnp
from jax import lax
from jax.sharding import PartitionSpec as P

D = 1024
ITERS = 2


LAMBDA = 0.001
EPSILON = 1e-06
HIGHEST = lax.Precision.HIGHEST


def kernel_tile(rows_data, landmarks, sq_lands):
    sq_rows = jnp.sum(jnp.square(rows_data.astype(jnp.float32)), axis=1)
    products = lax.dot_general(
        rows_data, landmarks, (((1,), (1,)), ((), ())), preferred_element_type=jnp.float32
    )
    return jnp.exp(-(sq_rows[:, None] + sq_lands[None, :] - 2.0 * products) / D)


def contract_rows(matrix, vectors):
    return lax.dot_general(
        matrix,
        vectors,
        (((0,), (0,)), ((), ())),
        precision=HIGHEST,
        preferred_element_type=jnp.float32,
    )


def times_matrix(matrix, vectors):
    return jnp.dot(matrix, vectors, precision=HIGHEST, preferred_element_type=jnp.float32)


def col_total(values):
    return lax.psum(values, "col")


def row_total(values):
    return lax.psum(values, "row")


def dot_total(values):
    return lax.psum(values, "col")


def column_sums(first, second):
    return jnp.sum(first * second, axis=0)


def shards(examples, targets, landmark_rows, ainv, tinv_t):
    row_count = lax.axis_size("row")
    total_rows = examples.shape[0] * row_count
    tile_width = landmark_rows.shape[0]
    owned_count = tile_width // row_count
    first_owned = lax.axis_index("row") * owned_count
    owned_ids = lax.dynamic_slice_in_dim(landmark_rows, first_owned, owned_count, 0)
    owned = jnp.take(examples, owned_ids, axis=0)
    landmarks = lax.all_gather(owned, "row", axis=0, tiled=True)
    sq_lands = jnp.sum(jnp.square(landmarks.astype(jnp.float32)), axis=1)
    kernel = kernel_tile(examples, landmarks, sq_lands)
    factor_a = ainv.reshape(-1, tile_width)
    factor_t = tinv_t.reshape(-1, tile_width)
    kernel_targets = row_total(contract_rows(kernel, targets))
    mixed = col_total(times_matrix(factor_t, kernel_targets))
    right_side = row_total(contract_rows(factor_a, mixed)) / math.sqrt(total_rows)
    solution = jnp.zeros(right_side.shape, jnp.float32)
    residual = right_side
    direction = right_side
    norm_now = dot_total(column_sums(residual, residual))
    for iteration in range(ITERS):
        mixed_in = col_total(times_matrix(factor_a, direction))
        lifted = row_total(contract_rows(factor_t, mixed_in))
        example_vals = lax.psum(times_matrix(kernel, lifted).astype(jnp.bfloat16), "col").astype(
            jnp.float32
        )
        local_back = contract_rows(kernel, example_vals)
        back = row_total(local_back)
        curvature = None
        lowered = col_total(times_matrix(factor_t, back))
        applied = row_total(contract_rows(factor_a, lowered / total_rows + LAMBDA * mixed_in))
        applied, curvature = (applied, curvature)
        step_size = norm_now / dot_total(column_sums(direction, applied))
        solution = solution + step_size * direction
        residual = residual - step_size * applied
        norm_next = dot_total(column_sums(residual, residual))
        direction = residual + norm_next / (norm_now + EPSILON) * direction
        norm_now = norm_next
    weights = row_total(contract_rows(factor_t, col_total(times_matrix(factor_a, solution))))
    return (solution, weights)


def solution(mesh):
    return jax.shard_map(
        shards,
        mesh=mesh,
        in_specs=(
            P("row", None),
            P("row", None),
            P("col"),
            P(None, "row", None, "col"),
            P(None, "row", None, "col"),
        ),
        out_specs=(P("col", None), P("col", None)),
        check_vma=False,
    )
```

profile of v0, /device:TPU:0, one launch (start us, length us, event | category | flops | bytes accessed | tf_op | source)
XLA Modules:
  0.0 1241.8 jit_solution(5362592691679920946)
XLA Ops:
  7.2 0.9 compare_and_fusion
  8.2 3.4 gather_fusion
  11.6 0.9 broadcast_select_fusion
  12.5 0.0 all-reduce.19.cloned.1.call-start
  12.6 2.1 multiply_reduce_fusion.1
  14.7 74.1 %all-gather.2.cloned.1.call-done = bf16[2048,1024]{1,0:T(8,128)(2,1)} async-done(((bf16[256,1024]{1,0:T(8,128)(2,1)}), bf16[2048,1024]{1,0:T(8,128)(2,1)}) %all-gather.2.cloned.1.call-update) | async-done | bytes 4194320 | tf_op jit(solution)/shard_map/all_gather | solution.py:63
  88.8 3.1 multiply_reduce_fusion
  91.9 6.9 fusion.2
  98.8 3.2 copy-done.1
  102.0 7.7 fusion.21
  109.7 0.3 all-reduce.21.cloned.1.call-start
  110.0 76.3 %all-reduce.19.cloned.1.call-done = f32[2048,64]{1,0:T(8,128)} async-done(((f32[2048,64]{1,0:T(8,128)}), f32[2048,64]{1,0:T(8,128)}) %all-reduce.19.cloned.1.call-update) | async-done | bytes 524304 | tf_op jit(solution)/shard_map/psum | solution.py:44
  186.3 12.7 %convolution_bitcast_fusion.11 = f32[1024,64]{0,1:T(8,128)} fusion(f32[2048,64]{1,0:T(8,128)} %all-reduce.19.cloned.1.call-done, f32[1024,2048]{1,0:T(8,128)} %bitcast.72), kind=kOutput, calls=%fused_computation.20 | convolution fusion | flops 1610612736 | bytes 9175040 | tf_op jit(solution)/shard_map/dot_general | solution.py:36
  199.0 0.0 all-reduce.23.cloned.1.call-start
  199.1 31.7 %all-reduce.21.cloned.1.call-done = f32[1024,64]{0,1:T(8,128)} async-done(((f32[1024,64]{0,1:T(8,128)}), f32[1024,64]{0,1:T(8,128)}) %all-reduce.21.cloned.1.call-update) | async-done | bytes 262160 | tf_op jit(solution)/shard_map/psum | solution.py:40
  230.7 9.4 convolution_bitcast_fusion.5
  240.2 0.4 all-reduce.25.cloned.1.call-start
  240.6 72.1 %all-reduce.23.cloned.1.call-done = f32[2048,64]{0,1:T(8,128)} async-done(((f32[2048,64]{0,1:T(8,128)}), f32[2048,64]{0,1:T(8,128)}) %all-reduce.23.cloned.1.call-update) | async-done | bytes 524304 | tf_op jit(solution)/shard_map/psum | solution.py:44
  312.7 12.3 convolution_bitcast_fusion.8
  325.0 0.0 all-reduce.27.cloned.1.call-start
  325.1 31.3 %all-reduce.25.cloned.1.call-done = f32[1024,64]{0,1:T(8,128)} async-done(((f32[1024,64]{0,1:T(8,128)}), f32[1024,64]{0,1:T(8,128)}) %all-reduce.25.cloned.1.call-update) | async-done | bytes 262160 | tf_op jit(solution)/shard_map/psum | solution.py:40
  356.4 9.4 convolution_bitcast_fusion.4
  365.8 0.2 all-reduce.29.cloned.1.call-start
  366.1 72.3 %all-reduce.27.cloned.1.call-done = f32[2048,64]{0,1:T(8,128)} async-done(((f32[2048,64]{0,1:T(8,128)}), f32[2048,64]{0,1:T(8,128)}) %all-reduce.27.cloned.1.call-update) | async-done | bytes 524304 | tf_op jit(solution)/shard_map/psum | solution.py:44
  438.4 16.3 %convolution_convert_fusion.1 = bf16[1024,64]{1,0:T(8,128)(2,1)} fusion(f32[1024,2048]{0,1:T(8,128)} %copy-done.1, f32[2048,64]{0,1:T(8,128)} %all-reduce.27.cloned.1.call-done), kind=kOutput, calls=%fused_computation.14 | convolution fusion | flops 1610678272 | bytes 9043968 | tf_op jit(solution)/shard_map/dot_general | solution.py:36
  454.7 0.0 all-reduce.31.cloned.1.call-start
  454.8 31.4 %all-reduce.29.cloned.1.call-done = bf16[1024,64]{1,0:T(8,128)(2,1)} async-done(((bf16[1024,64]{1,0:T(8,128)(2,1)}), bf16[1024,64]{1,0:T(8,128)(2,1)}) %all-reduce.29.cloned.1.call-update) | async-done | bytes 131088 | tf_op jit(solution)/shard_map/psum | solution.py:78
  486.1 8.2 fusion.22
  494.4 0.3 all-reduce.33.cloned.1.call-start
  494.7 78.0 %all-reduce.31.cloned.1.call-done = f32[2048,64]{1,0:T(8,128)} async-done(((f32[2048,64]{1,0:T(8,128)}), f32[2048,64]{1,0:T(8,128)}) %all-reduce.31.cloned.1.call-update) | async-done | bytes 524304 | tf_op jit(solution)/shard_map/psum | solution.py:44
  572.7 12.7 %convolution_bitcast_fusion.10 = f32[1024,64]{0,1:T(8,128)} fusion(f32[2048,64]{1,0:T(8,128)} %all-reduce.31.cloned.1.call-done, f32[1024,2048]{1,0:T(8,128)} %bitcast.74), kind=kOutput, calls=%fused_computation.19 | convolution fusion | flops 1610612736 | bytes 9175040 | tf_op jit(solution)/shard_map/dot_general | solution.py:36
  585.5 0.0 all-reduce.35.cloned.1.call-start
  585.5 31.6 %all-reduce.33.cloned.1.call-done = f32[1024,64]{0,1:T(8,128)} async-done(((f32[1024,64]{0,1:T(8,128)}), f32[1024,64]{0,1:T(8,128)}) %all-reduce.33.cloned.1.call-update) | async-done | bytes 262160 | tf_op jit(solution)/shard_map/psum | solution.py:40
  617.2 9.4 convolution_bitcast_fusion.3
  626.6 0.0 all-reduce.37.cloned.1.call-start
  626.6 72.5 %all-reduce.35.cloned.1.call-done = f32[2048,64]{0,1:T(8,128)} async-done(((f32[2048,64]{0,1:T(8,128)}), f32[2048,64]{0,1:T(8,128)}) %all-reduce.35.cloned.1.call-update) | async-done | bytes 524304 | tf_op jit(solution)/shard_map/psum | solution.py:44
  699.1 1.2 multiply_reduce_fusion.4
  700.3 5.7 all-reduce
  706.0 1.3 multiply_reduce_fusion.3
  707.3 7.0 psum.158
  714.3 12.4 convolution_bitcast_fusion.7
  726.8 0.0 all-reduce.39.cloned.1.call-start
  726.8 30.8 %all-reduce.37.cloned.1.call-done = f32[1024,64]{0,1:T(8,128)} async-done(((f32[1024,64]{0,1:T(8,128)}), f32[1024,64]{0,1:T(8,128)}) %all-reduce.37.cloned.1.call-update) | async-done | bytes 262160 | tf_op jit(solution)/shard_map/psum | solution.py:40
  757.6 9.4 convolution_bitcast_fusion.2
  767.0 0.2 all-reduce.41.cloned.1.call-start
  767.2 72.2 %all-reduce.39.cloned.1.call-done = f32[2048,64]{0,1:T(8,128)} async-done(((f32[2048,64]{0,1:T(8,128)}), f32[2048,64]{0,1:T(8,128)}) %all-reduce.39.cloned.1.call-update) | async-done | bytes 524304 | tf_op jit(solution)/shard_map/psum | solution.py:44
  839.5 16.3 %convolution_convert_fusion = bf16[1024,64]{1,0:T(8,128)(2,1)} fusion(f32[1024,2048]{0,1:T(8,128)} %copy-done.1, f32[2048,64]{0,1:T(8,128)} %all-reduce.39.cloned.1.call-done), kind=kOutput, calls=%fused_computation.13 | convolution fusion | flops 1610678272 | bytes 9043968 | tf_op jit(solution)/shard_map/dot_general | solution.py:36
  855.8 0.0 all-reduce.43.cloned.1.call-start
  855.9 31.4 %all-reduce.41.cloned.1.call-done = bf16[1024,64]{1,0:T(8,128)(2,1)} async-done(((bf16[1024,64]{1,0:T(8,128)(2,1)}), bf16[1024,64]{1,0:T(8,128)(2,1)}) %all-reduce.41.cloned.1.call-update) | async-done | bytes 131088 | tf_op jit(solution)/shard_map/psum | solution.py:78
  887.2 8.2 fusion.23
  895.5 0.3 all-reduce.45.cloned.1.call-start
  895.8 78.0 %all-reduce.43.cloned.1.call-done = f32[2048,64]{1,0:T(8,128)} async-done(((f32[2048,64]{1,0:T(8,128)}), f32[2048,64]{1,0:T(8,128)}) %all-reduce.43.cloned.1.call-update) | async-done | bytes 524304 | tf_op jit(solution)/shard_map/psum | solution.py:44
  973.8 12.7 %convolution_bitcast_fusion.9 = f32[1024,64]{0,1:T(8,128)} fusion(f32[2048,64]{1,0:T(8,128)} %all-reduce.43.cloned.1.call-done, f32[1024,2048]{1,0:T(8,128)} %bitcast.76), kind=kOutput, calls=%fused_computation.18 | convolution fusion | flops 1610612736 | bytes 9175040 | tf_op jit(solution)/shard_map/dot_general | solution.py:36
  986.6 31.7 %all-reduce.45.cloned.1.call-done = f32[1024,64]{0,1:T(8,128)} async-done(((f32[1024,64]{0,1:T(8,128)}), f32[1024,64]{0,1:T(8,128)}) %all-reduce.45.cloned.1.call-update) | async-done | bytes 262160 | tf_op jit(solution)/shard_map/psum | solution.py:40
  1018.2 9.4 convolution_bitcast_fusion.1
  1027.7 72.5 %all-reduce.47.cloned.1.call-done = f32[2048,64]{0,1:T(8,128)} async-done(((f32[2048,64]{0,1:T(8,128)}), f32[2048,64]{0,1:T(8,128)}) %all-reduce.47.cloned.1.call-update) | async-done | bytes 524304 | tf_op jit(solution)/shard_map/psum | solution.py:44
  1100.2 1.3 multiply_reduce_fusion.2
  1101.6 5.9 psum.165
  1107.5 0.3 multiply_add_fusion
  1107.8 11.3 convolution_bitcast_fusion.6
  1119.1 31.5 %all-reduce.49.cloned.1.call-done = f32[1024,64]{0,1:T(8,128)} async-done(((f32[1024,64]{0,1:T(8,128)}), f32[1024,64]{0,1:T(8,128)}) %all-reduce.49.cloned.1.call-update) | async-done | bytes 262160 | tf_op jit(solution)/shard_map/psum | solution.py:40
  1150.7 9.4 convolution_bitcast_fusion
  1160.1 72.6 %all-reduce.51.cloned.1.call-done = f32[2048,64]{0,1:T(8,128)} async-done(((f32[2048,64]{0,1:T(8,128)}), f32[2048,64]{0,1:T(8,128)}) %all-reduce.51.cloned.1.call-update) | async-done | bytes 524304 | tf_op jit(solution)/shard_map/psum | solution.py:44
  1232.7 1.9 copy.24
  (41 shorter events, 0.5 us)
Async XLA Ops:
  7.2 94.8 %copy-start = (f32[1024,64]{0,1:T(8,128)S(1)}, f32[1024,64]{0,1:T(8,128)}, u32[]{:S(2)}) copy-start(f32[1024,64]{0,1:T(8,128)} %param.6) | copy-start | bytes 786436
  7.2 84.7 %copy-start.3 = (bf16[1024,1024]{1,0:T(8,128)(2,1)S(1)}, bf16[1024,1024]{1,0:T(8,128)(2,1)}, u32[]{:S(2)}) copy-start(bf16[1024,1024]{1,0:T(8,128)(2,1)} %param.5) | copy-start | bytes 6291460
  7.2 81.6 %all-gather.2.cloned.1.call-start = ((), (), s32[]{:S(2)}) async-start(), calls=%async_computation | async-start | bytes 4718592 | tf_op jit(solution)/shard_map/all_gather | solution.py:63
  12.5 173.8 %all-reduce.19.cloned.1.call-start = ((), (), s32[]{:S(2)}) async-start(), calls=%async_computation.1 | async-start | bytes 2097152 | tf_op jit(solution)/shard_map/psum | solution.py:44
  98.7 3.2 copy-start.1
  109.7 121.0 %all-reduce.21.cloned.1.call-start = ((), (), s32[]{:S(2)}) async-start(), calls=%async_computation.2 | async-start | bytes 524288 | tf_op jit(solution)/shard_map/psum | solution.py:40
  199.0 113.7 %all-reduce.23.cloned.1.call-start = ((), (), s32[]{:S(2)}) async-start(), calls=%async_computation.3 | async-start | bytes 1048576 | tf_op jit(solution)/shard_map/psum | solution.py:44
  240.2 116.2 %all-reduce.25.cloned.1.call-start = ((), (), s32[]{:S(2)}) async-start(), calls=%async_computation.4 | async-start | bytes 524288 | tf_op jit(solution)/shard_map/psum | solution.py:40
  325.0 113.4 %all-reduce.27.cloned.1.call-start = ((), (), s32[]{:S(2)}) async-start(), calls=%async_computation.5 | async-start | bytes 1048576 | tf_op jit(solution)/shard_map/psum | solution.py:44
  365.8 120.3 %all-reduce.29.cloned.1.call-start = ((), (), s32[]{:S(2)}) async-start(), calls=%async_computation.6 | async-start | bytes 524288 | tf_op jit(solution)/shard_map/psum | solution.py:78
  454.7 162.4 %copy-start.7 = (f32[1024,64]{0,1:T(8,128)S(1)}, f32[1024,64]{0,1:T(8,128)}, u32[]{:S(2)}) copy-start(f32[1024,64]{0,1:T(8,128)} %all-reduce.25.cloned.1.call-done) | copy-start | bytes 786436
  454.7 118.0 %all-reduce.31.cloned.1.call-start = ((), (), s32[]{:S(2)}) async-start(), calls=%async_computation.7 | async-start | bytes 2097152 | tf_op jit(solution)/shard_map/psum | solution.py:44
  494.4 204.7 %copy-start.2 = (f32[2048,64]{0,1:T(8,128)S(1)}, f32[2048,64]{0,1:T(8,128)}, u32[]{:S(2)}) copy-start(f32[2048,64]{0,1:T(8,128)} %all-reduce.23.cloned.1.call-done) | copy-start | bytes 1572868
  494.4 122.8 %all-reduce.33.cloned.1.call-start = ((), (), s32[]{:S(2)}) async-start(), calls=%async_computation.8 | async-start | bytes 524288 | tf_op jit(solution)/shard_map/psum | solution.py:40
  585.5 113.6 %all-reduce.35.cloned.1.call-start = ((), (), s32[]{:S(2)}) async-start(), calls=%async_computation.9 | async-start | bytes 1048576 | tf_op jit(solution)/shard_map/psum | solution.py:44
  626.6 131.0 %all-reduce.37.cloned.1.call-start = ((), (), s32[]{:S(2)}) async-start(), calls=%async_computation.10 | async-start | bytes 524288 | tf_op jit(solution)/shard_map/psum | solution.py:40
  726.8 112.7 %all-reduce.39.cloned.1.call-start = ((), (), s32[]{:S(2)}) async-start(), calls=%async_computation.11 | async-start | bytes 1048576 | tf_op jit(solution)/shard_map/psum | solution.py:44
  767.0 120.2 %all-reduce.41.cloned.1.call-start = ((), (), s32[]{:S(2)}) async-start(), calls=%async_computation.12 | async-start | bytes 524288 | tf_op jit(solution)/shard_map/psum | solution.py:78
  855.8 162.4 %copy-start.6 = (f32[1024,64]{0,1:T(8,128)S(1)}, f32[1024,64]{0,1:T(8,128)}, u32[]{:S(2)}) copy-start(f32[1024,64]{0,1:T(8,128)} %all-reduce.37.cloned.1.call-done) | copy-start | bytes 786436
  855.8 118.0 %all-reduce.43.cloned.1.call-start = ((), (), s32[]{:S(2)}) async-start(), calls=%async_computation.13 | async-start | bytes 2097152 | tf_op jit(solution)/shard_map/psum | solution.py:44
  895.5 204.7 %copy-start.4 = (f32[2048,64]{0,1:T(8,128)S(1)}, f32[2048,64]{0,1:T(8,128)}, u32[]{:S(2)}) copy-start(f32[2048,64]{0,1:T(8,128)} %all-reduce.35.cloned.1.call-done) | copy-start | bytes 1572868
  895.5 122.7 %all-reduce.45.cloned.1.call-start = ((), (), s32[]{:S(2)}) async-start(), calls=%async_computation.14 | async-start | bytes 524288 | tf_op jit(solution)/shard_map/psum | solution.py:40
  986.5 113.7 %all-reduce.47.cloned.1.call-start = ((), (), s32[]{:S(2)}) async-start(), calls=%async_computation.15 | async-start | bytes 1048576 | tf_op jit(solution)/shard_map/psum | solution.py:44
  1027.7 123.0 %all-reduce.49.cloned.1.call-start = ((), (), s32[]{:S(2)}) async-start(), calls=%async_computation.16 | async-start | bytes 524288 | tf_op jit(solution)/shard_map/psum | solution.py:40
  1107.8 52.3 %copy-start.5 = (f32[2048,64]{0,1:T(8,128)}, f32[2048,64]{0,1:T(8,128)S(1)}, u32[]{:S(2)}) copy-start(f32[2048,64]{0,1:T(8,128)S(1)} %multiply_add_fusion) | copy-start | bytes 1572868
  1119.1 113.6 %all-reduce.51.cloned.1.call-start = ((), (), s32[]{:S(2)}) async-start(), calls=%async_computation.17 | async-start | bytes 1048576 | tf_op jit(solution)/shard_map/psum | solution.py:44
Sparse Core Ops, SparseCore 0:
  12.7 76.0 all-gather.1
  109.9 76.3 all-reduce.18
  199.2 31.5 all-reduce.20
  240.3 72.3 all-reduce.22
  325.1 31.2 all-reduce.24
  366.0 72.3 all-reduce.26
  454.8 31.2 all-reduce.28
  494.5 78.1 all-reduce.30
  585.6 31.5 all-reduce.32
  626.7 72.3 all-reduce.34
  726.9 30.6 all-reduce.36
  767.1 72.3 all-reduce.38
  855.9 31.2 all-reduce.40
  895.6 78.1 all-reduce.42
  986.6 31.5 all-reduce.44
  1027.8 72.3 all-reduce.46
  1119.2 31.4 all-reduce.48
  1160.2 72.3 all-reduce.50
where the time goes:
time: 1250 us; the launch traced here: 1240 us
  waiting for transfers between devices  992 us (79%)
  matrix products  194 us (16%)
  blocking collectives  18.6 us (1%)
  between operations  14.9 us (1%)
    psum x9, waiting for transfers between devices, row_total(): return lax.psum(values, 'row')  667 us
    psum x6, waiting for transfers between devices, col_total(): return lax.psum(values, 'col')  189 us
    dot_general x8, matrix products, times_matrix(): jnp.dot(matrix, vectors, precision=HIGHEST, preferred_element_type=jnp.fl...  107 us
    dot_general x9, matrix products, contract_rows(): lax.dot_general(matrix, vectors, (((0,), (0,)), ((), ())), precision=HIGH...  80.7 us
    all_gather x1, waiting for transfers between devices, shards(): landmarks = lax.all_gather(owned, 'row', axis=0, tiled=True)  74.1 us
    psum x2, waiting for transfers between devices, shards(): lax.psum(times_matrix(kernel, lifted).astype(jnp.bfloat16), 'col')  62.7 us
  transfers between devices with their start and end apart: 18, of which 18 were waited for; matrix products, arithmetic and copies ran while one was open for 0% of the time, Pallas kernels for 0%

commit v1 on v0

v1 whole, which is shorter than its diff:
```python
import functools
import math

import jax
import jax.numpy as jnp
from jax import lax
from jax.experimental import pallas as pl
from jax.experimental.pallas import tpu as pltpu
from jax.sharding import PartitionSpec as P

D = 1024
LAMBDA = 0.001
EPSILON = 1e-06
F32 = jnp.float32
BF16 = jnp.bfloat16
MESH = pl.DeviceIdType.MESH


def greet(axis, me, n):
    barrier = pltpu.get_barrier_semaphore()

    def hello(s, carry):
        pl.semaphore_signal(
            barrier, inc=1, device_id={axis: lax.rem(me + s, n)}, device_id_type=MESH
        )
        return carry

    lax.fori_loop(1, n, hello, 0)
    pl.semaphore_wait(barrier, n - 1)


def square_sums(values):
    return jnp.broadcast_to(
        jnp.sum(values * values, axis=1, keepdims=True), (values.shape[0], 128)
    )


def product_kernel(
    axis, n, contract, mat, vec, out, sq_out, send, recv, gath, sq, split,
    s1, r1, s2, r2, s3, r3,
):
    me = lax.axis_index(axis)
    c = vec.shape[0]
    w = send.shape[2]

    def to_peer(src, dst, ssem, rsem, peer):
        return pltpu.make_async_remote_copy(
            src_ref=src, dst_ref=dst, send_sem=ssem, recv_sem=rsem,
            device_id={axis: peer}, device_id_type=MESH,
        )

    values = vec[...]
    high = values.astype(BF16)
    split[0:c, :] = high
    split[c:, :] = (values - high.astype(F32)).astype(BF16)
    sq[me] = square_sums(values)
    greet(axis, me, n)

    def chunk_product(j):
        if contract:
            start = j * w if isinstance(j, int) else pl.multiple_of(j * w, 128)
            m = mat[:, pl.ds(start, w)]
            dims = (((1,), (0,)), ((), ()))
        else:
            start = j * w if isinstance(j, int) else pl.multiple_of(j * w, 8)
            m = mat[pl.ds(start, w), :]
            dims = (((1,), (1,)), ((), ()))
        m_high = m.astype(BF16)
        m_low = (m - m_high.astype(F32)).astype(BF16)
        both = lax.dot_general(split[...], m_high, dims, preferred_element_type=F32)
        rest = lax.dot_general(split[0:c, :], m_low, dims, preferred_element_type=F32)
        return both[0:c] + (both[c:] + rest)

    aligned = w % 128 == 0
    if not aligned:
        for j in range(n):
            send[j] = chunk_product(j)

    def first(s, carry):
        peer = lax.rem(me + s, n)
        if aligned:
            send[peer] = chunk_product(peer)
        to_peer(send.at[peer], recv.at[s], s1.at[s], r1.at[s], peer).start()
        to_peer(sq.at[me], sq.at[me], s3.at[s], r3.at[s], peer).start()
        return carry

    lax.fori_loop(1, n, first, 0)
    if aligned:
        send[me] = chunk_product(me)

    def gather_in(s, total):
        to_peer(send.at[0], recv.at[s], s1.at[s], r1.at[s], lax.rem(me + s, n)).wait_recv()
        return total + recv[s]

    gath[me] = lax.fori_loop(1, n, gather_in, send[me])

    def second(s, carry):
        peer = lax.rem(me + s, n)
        to_peer(gath.at[me], gath.at[me], s2.at[s], r2.at[s], peer).start()
        return carry

    lax.fori_loop(1, n, second, 0)

    def finish(s, carry):
        source = lax.rem(me + n - s, n)
        to_peer(sq.at[me], sq.at[source], s3.at[s], r3.at[s], lax.rem(me + s, n)).wait()
        to_peer(gath.at[me], gath.at[source], s2.at[s], r2.at[s], lax.rem(me + s, n)).wait()
        to_peer(send.at[0], recv.at[s], s1.at[s], r1.at[s], lax.rem(me + s, n)).wait_send()
        return carry

    lax.fori_loop(1, n, finish, 0)
    total = sq[0]
    for j in range(1, n):
        total = total + sq[j]
    sq_out[...] = total
    for j in range(n):
        out[:, j * w : (j + 1) * w] = gath[j]


def product(axis, contract, ident, mat, vec):
    n = lax.axis_size(axis)
    c = vec.shape[0]
    length = mat.shape[1] if contract else mat.shape[0]
    depth = mat.shape[0] if contract else mat.shape[1]
    w = length // n
    vmem = pl.BlockSpec(memory_space=pltpu.VMEM)
    out, sq = pl.pallas_call(
        functools.partial(product_kernel, axis, n, contract),
        out_shape=(
            jax.ShapeDtypeStruct((c, length), F32),
            jax.ShapeDtypeStruct((c, 128), F32),
        ),
        in_specs=[vmem, vmem],
        out_specs=(vmem, vmem),
        scratch_shapes=[
            pltpu.VMEM((n, c, w), F32),
            pltpu.VMEM((n, c, w), F32),
            pltpu.VMEM((n, c, w), F32),
            pltpu.VMEM((n, c, 128), F32),
            pltpu.VMEM((2 * c, depth), BF16),
        ]
        + [pltpu.SemaphoreType.DMA((n,))] * 6,
        compiler_params=pltpu.CompilerParams(
            collective_id=ident, has_side_effects=True, vmem_limit_bytes=48 * 2**20
        ),
    )(mat, vec)
    return out, sq[:, 0:1]


def square_kernel(axis, n, vec, sq_out, sq, s3, r3):
    me = lax.axis_index(axis)
    sq[me] = square_sums(vec[...])
    greet(axis, me, n)

    def copy(s, slot, peer):
        return pltpu.make_async_remote_copy(
            src_ref=sq.at[me], dst_ref=sq.at[slot], send_sem=s3.at[s], recv_sem=r3.at[s],
            device_id={axis: peer}, device_id_type=MESH,
        )

    def start(s, carry):
        copy(s, me, lax.rem(me + s, n)).start()
        return carry

    def finish(s, carry):
        copy(s, lax.rem(me + n - s, n), lax.rem(me + s, n)).wait()
        return carry

    lax.fori_loop(1, n, start, 0)
    lax.fori_loop(1, n, finish, 0)
    total = sq[0]
    for j in range(1, n):
        total = total + sq[j]
    sq_out[...] = total


def square_total(axis, ident, vec):
    n = lax.axis_size(axis)
    c = vec.shape[0]
    vmem = pl.BlockSpec(memory_space=pltpu.VMEM)
    return pl.pallas_call(
        functools.partial(square_kernel, axis, n),
        out_shape=jax.ShapeDtypeStruct((c, 128), F32),
        in_specs=[vmem],
        out_specs=vmem,
        scratch_shapes=[pltpu.VMEM((n, c, 128), F32)] + [pltpu.SemaphoreType.DMA((n,))] * 2,
        compiler_params=pltpu.CompilerParams(collective_id=ident, has_side_effects=True),
    )(vec)[:, 0:1]


def kernel_tile(rows_data, landmarks):
    sq_lands = jnp.sum(jnp.square(landmarks.astype(F32)), axis=1)
    sq_rows = jnp.sum(jnp.square(rows_data.astype(F32)), axis=1)
    products = lax.dot_general(
        rows_data, landmarks, (((1,), (1,)), ((), ())), preferred_element_type=F32
    )
    return jnp.exp(-(sq_rows[:, None] + sq_lands[None, :] - 2.0 * products) / D)


def shards(examples, targets, landmark_rows, ainv, tinv_t):
    row_count = lax.axis_size("row")
    total_rows = examples.shape[0] * row_count
    tile_width = landmark_rows.shape[0]
    owned_count = tile_width // row_count
    first_owned = lax.axis_index("row") * owned_count
    owned_ids = lax.dynamic_slice_in_dim(landmark_rows, first_owned, owned_count, 0)
    owned = jnp.take(examples, owned_ids, axis=0)
    landmarks = lax.all_gather(owned, "row", axis=0, tiled=True)
    kernel = kernel_tile(examples, landmarks)
    factor_a = ainv.reshape(-1, tile_width)
    factor_t = tinv_t.reshape(-1, tile_width)

    kernel_back = functools.partial(product, "row", True, 0, kernel)
    kernel_on = functools.partial(product, "col", False, 1, kernel)
    factor_back = functools.partial(product, "row", True, 2)
    factor_on = functools.partial(product, "col", False, 3)

    kernel_targets, _ = kernel_back(targets.T)
    mixed, _ = factor_on(factor_t, kernel_targets)
    right_side, _ = factor_back(factor_a, mixed)
    right_side = right_side / math.sqrt(total_rows)

    mixed_0, norm_0 = factor_on(factor_a, right_side)
    lifted_0, mixed_sq = factor_back(factor_t, mixed_0)
    example_vals, _ = kernel_on(lifted_0)
    back, vals_sq = kernel_back(example_vals)
    step_0 = norm_0 / (vals_sq / total_rows + LAMBDA * mixed_sq)
    lowered, _ = factor_on(factor_t, back)
    applied, _ = factor_back(factor_a, lowered / total_rows + LAMBDA * mixed_0)
    residual = right_side - step_0 * applied

    mixed_r, norm_1 = factor_on(factor_a, residual)
    ratio = norm_1 / (norm_0 + EPSILON)
    direction = residual + ratio * right_side
    lifted_1, mixed_sq = factor_back(factor_t, mixed_r + ratio * mixed_0)
    example_vals, _ = kernel_on(lifted_1)
    vals_sq = square_total("row", 4, example_vals)
    step_1 = norm_1 / (vals_sq / total_rows + LAMBDA * mixed_sq)
    solution = step_0 * right_side + step_1 * direction
    weights = step_0 * lifted_0 + step_1 * lifted_1
    return (solution.T, weights.T)


def solution(mesh):
    return jax.shard_map(
        shards,
        mesh=mesh,
        in_specs=(
            P("row", None),
            P("row", None),
            P("col"),
            P(None, "row", None, "col"),
            P(None, "row", None, "col"),
        ),
        out_specs=(P("col", None), P("col", None)),
        check_vma=False,
    )
```

time: 1250 us -> 445 us (0.36)
  waiting for transfers between devices: 992 us -> 74.2 us
  Pallas kernels: 0 us -> 333 us
  matrix products: 194 us -> 9.8 us
  blocking collectives: 18.6 us -> 0 us
    psum x17 -> x0, waiting for transfers between devices: 918 us -> none  [the longest x9 667 us: row_total(): return lax.psum(values, 'row')]
    pallas_call x0 -> x13, Pallas kernels: none -> 333 us  [the longest x12 318 us: product(): pl.pallas_call(functools.partial(product_kernel, axis, n, contract), out_...]
    dot_general x17 -> x0, matrix products: 187 us -> none  [the longest x8 107 us: times_matrix(): jnp.dot(matrix, vectors, precision=HIGHEST, preferred_element_type=jnp.fl...]
    psum x3 -> x0, blocking collectives: 18.6 us -> none  [dot_total(): return lax.psum(values, 'col')]
  transfers between devices with their start and end apart: 18 -> 1, of which waited for: 18 -> 1; matrix products, arithmetic and copies ran while one was open for 0% -> 0% of each run, Pallas kernels for 0% -> 0%
where the time goes in v1:
time: 445 us
  Pallas kernels  333 us (75%)
  waiting for transfers between devices  74.2 us (17%)
  between operations  14.2 us (3%)
  matrix products  9.8 us (2%)
  other arithmetic  9.59 us (2%)
    pallas_call x12, Pallas kernels, product(): pl.pallas_call(functools.partial(product_kernel, axis, n, contract), out_...  318 us
    all_gather x1, waiting for transfers between devices, shards(): landmarks = lax.all_gather(owned, 'row', axis=0, tiled=True)  74.2 us
    pallas_call x1, Pallas kernels, square_total(): pl.pallas_call(functools.partial(square_kernel, axis, n), out_shape=jax.S...  14.6 us
    dot_general x1, matrix products, kernel_tile(): lax.dot_general(rows_data, landmarks, (((1,), (1,)), ((), ())), preferred...  9.8 us
  transfers between devices with their start and end apart: 1, of which 1 were waited for; matrix products, arithmetic and copies ran while one was open for 0% of the time, Pallas kernels for 0%

profile of v1, /device:TPU:0, one launch (start us, length us, event | category | flops | bytes accessed | tf_op | source)
XLA Modules:
  0.0 444.6 jit_solution(9988105034139402014)
XLA Ops:
  7.2 0.0 copy-start.2
  7.2 0.0 all-gather.2.cloned.1.call-start
  7.2 0.9 compare_and_fusion
  8.1 3.4 gather_fusion
  11.6 0.9 broadcast_select_fusion
  12.5 0.0 all-gather.2.cloned.1.call-update
  12.5 2.1 multiply_reduce_fusion.1
  14.6 74.2 %all-gather.2.cloned.1.call-done = bf16[2048,1024]{1,0:T(8,128)(2,1)} async-done(((bf16[256,1024]{1,0:T(8,128)(2,1)}), bf16[2048,1024]{1,0:T(8,128)(2,1)}) %all-gather.2.cloned.1.call-update) | async-done | bytes 4194320 | tf_op jit(solution)/shard_map/all_gather | solution.py:208
  88.8 3.1 multiply_reduce_fusion
  91.8 0.0 copy-done.2
  91.8 0.0 copy-start
  91.9 9.8 %fusion.2.mat = f32[1024,2048]{1,0:T(8,128)} fusion(bf16[2048,1024]{1,0:T(8,128)(2,1)} %all-gather.2.cloned.1.call-done, bf16[1024,1024]{1,0:T(8,128)(2,1)S(1)} %copy-done.2, f32[2048]{0:T(1024)S(1)} %multiply_reduce_fusion, f32[1024]{0:T(1024)S(1)} %multiply_reduce_fusion.1), kind=kOutput, calls=%fused_computation.4 | convolution fusion | flops 4305453056 | bytes 14692352 | tf_op jit(solution)/shard_map/dot_general | solution.py:194
  101.7 0.0 copy-done
  101.7 35.6 %shard_map.68 = (f32[64,2048]{1,0:T(8,128)S(1)}, f32[64,128]{1,0:T(8,128)}) custom-call(f32[1024,2048]{1,0:T(8,128)} %fusion.2.mat, f32[64,1024]{1,0:T(8,128)S(1)} %bitcast.17), custom_call_target="tpu_custom_call" | custom-call | tf_op jit(solution)/shard_map/pallas_call | solution.py:127
  137.3 15.6 %shard_map.69 = (f32[64,1024]{1,0:T(8,128)S(1)}, f32[64,128]{1,0:T(8,128)}) custom-call(f32[1024,2048]{1,0:T(8,128)} %bitcast.22, f32[64,2048]{1,0:T(8,128)S(1)} %get-tuple-element.19.vec), custom_call_target="tpu_custom_call" | custom-call | tf_op jit(solution)/shard_map/pallas_call | solution.py:127
  153.0 36.6 %shard_map.70 = (f32[64,2048]{1,0:T(8,128)S(1)}, f32[64,128]{1,0:T(8,128)}) custom-call(f32[1024,2048]{1,0:T(8,128)} %bitcast.18, f32[64,1024]{1,0:T(8,128)S(1)} %get-tuple-element.20.vec), custom_call_target="tpu_custom_call" | custom-call | tf_op jit(solution)/shard_map/pallas_call | solution.py:127
  189.6 14.1 %shard_map.71 = (f32[64,1024]{1,0:T(8,128)S(1)}, f32[64,128]{1,0:T(8,128)S(1)}) custom-call(f32[1024,2048]{1,0:T(8,128)} %bitcast.19, f32[64,2048]{1,0:T(8,128)S(1)} %broadcast_multiply_fusion.vec), custom_call_target="tpu_custom_call" | custom-call | tf_op jit(solution)/shard_map/pallas_call | solution.py:127
  203.8 38.9 %shard_map.72 = (f32[64,2048]{1,0:T(8,128)S(1)}, f32[64,128]{1,0:T(8,128)S(1)}) custom-call(f32[1024,2048]{1,0:T(8,128)} %bitcast.23, f32[64,1024]{1,0:T(8,128)S(1)} %get-tuple-element.23.vec), custom_call_target="tpu_custom_call" | custom-call | tf_op jit(solution)/shard_map/pallas_call | solution.py:127
  242.6 15.6 %shard_map.73 = (f32[64,1024]{1,0:T(8,128)S(1)}, f32[64,128]{1,0:T(8,128)}) custom-call(f32[1024,2048]{1,0:T(8,128)} %fusion.2.mat, f32[64,2048]{1,0:T(8,128)S(1)} %get-tuple-element.24.vec), custom_call_target="tpu_custom_call" | custom-call | tf_op jit(solution)/shard_map/pallas_call | solution.py:127
  258.3 38.8 %shard_map.74 = (f32[64,2048]{1,0:T(8,128)S(1)}, f32[64,128]{1,0:T(8,128)S(1)}) custom-call(f32[1024,2048]{1,0:T(8,128)} %fusion.2.mat, f32[64,1024]{1,0:T(8,128)S(1)} %get-tuple-element.25.vec), custom_call_target="tpu_custom_call" | custom-call | tf_op jit(solution)/shard_map/pallas_call | solution.py:127
  297.0 14.7 %shard_map.75 = (f32[64,1024]{1,0:T(8,128)S(1)}, f32[64,128]{1,0:T(8,128)}) custom-call(f32[1024,2048]{1,0:T(8,128)} %bitcast.24, f32[64,2048]{1,0:T(8,128)S(1)} %get-tuple-element.28.vec), custom_call_target="tpu_custom_call" | custom-call | tf_op jit(solution)/shard_map/pallas_call | solution.py:127
  311.8 39.4 %shard_map.76 = (f32[64,2048]{1,0:T(8,128)S(1)}, f32[64,128]{1,0:T(8,128)}) custom-call(f32[1024,2048]{1,0:T(8,128)} %bitcast.20, f32[64,1024]{1,0:T(8,128)S(1)} %multiply_add_fusion.1.vec), custom_call_target="tpu_custom_call" | custom-call | tf_op jit(solution)/shard_map/pallas_call | solution.py:127
  351.3 0.1 fusion.4
  351.4 0.1 multiply_subtract_fusion.vec
  351.5 15.0 %shard_map.77 = (f32[64,1024]{1,0:T(8,128)S(1)}, f32[64,128]{1,0:T(8,128)S(1)}) custom-call(f32[1024,2048]{1,0:T(8,128)} %bitcast.21, f32[64,2048]{1,0:T(8,128)S(1)} %multiply_subtract_fusion.vec), custom_call_target="tpu_custom_call" | custom-call | tf_op jit(solution)/shard_map/pallas_call | solution.py:127
  366.5 0.1 fusion.3
  366.7 0.1 multiply_add_fusion.vec
  366.8 38.8 %shard_map.78 = (f32[64,2048]{1,0:T(8,128)S(1)}, f32[64,128]{1,0:T(8,128)S(1)}) custom-call(f32[1024,2048]{1,0:T(8,128)} %bitcast.25, f32[64,1024]{1,0:T(8,128)S(1)} %multiply_add_fusion.vec), custom_call_target="tpu_custom_call" | custom-call | tf_op jit(solution)/shard_map/pallas_call | solution.py:127
  405.6 14.7 %shard_map.79 = (f32[64,1024]{1,0:T(8,128)S(1)}, f32[64,128]{1,0:T(8,128)}) custom-call(f32[1024,2048]{1,0:T(8,128)} %fusion.2.mat, f32[64,2048]{1,0:T(8,128)S(1)} %get-tuple-element.33.vec), custom_call_target="tpu_custom_call" | custom-call | tf_op jit(solution)/shard_map/pallas_call | solution.py:127
  420.3 0.0 copy-start.1
  420.3 0.7 copy-done.1
  421.0 14.6 %shard_map.80 = f32[64,128]{1,0:T(8,128)} custom-call(f32[64,1024]{1,0:T(8,128)} %copy-done.1), custom_call_target="tpu_custom_call" | custom-call | tf_op jit(solution)/shard_map/pallas_call | solution.py:181
  435.6 0.9 fusion.5
  436.5 1.2 add_bitcast_fusion
  (4 shorter events, 0.1 us)
Async XLA Ops:
  7.2 84.7 %copy-start.2 = (bf16[1024,1024]{1,0:T(8,128)(2,1)S(1)}, bf16[1024,1024]{1,0:T(8,128)(2,1)}, u32[]{:S(2)}) copy-start(bf16[1024,1024]{1,0:T(8,128)(2,1)} %param.5) | copy-start | bytes 6291460
  7.2 81.6 %all-gather.2.cloned.1.call-start = ((), (), s32[]{:S(2)}) async-start(), calls=%async_computation | async-start | bytes 4718592 | tf_op jit(solution)/shard_map/all_gather | solution.py:208
  91.8 9.8 %copy-start = (f32[1024,64]{0,1:T(8,128)S(1)}, f32[1024,64]{0,1:T(8,128)}, u32[]{:S(2)}) copy-start(f32[1024,64]{0,1:T(8,128)} %param.6) | copy-start | bytes 786436
  420.3 0.7 copy-start.1
Sparse Core Ops, SparseCore 0:
  12.6 76.0 all-gather.1
